TPU v7x, 256 devices: a whole 4x4x8 slice. The times are simulated.
256 devices in a mesh: row: 32 (over x, z), col: 8 (over y, core).
Axes of the slice: x: 4, y: 4, z: 8, core: 2. Of those that a mesh axis runs over, the one named last changes fastest.
Arguments:
- momentum: float32 [5120, 13312], P('row', 'col')
- gradient: float32 [5120, 13312], P('row', 'col'), may hold values from -6 to 6
Outputs:
- new_momentum: float32 [5120, 13312], P('row', 'col')
- update: float32 [5120, 13312], P('row', 'col')
All inputs are finite; a program needn't handle non-finite values.
Results may differ from a plain program's by a relative error of at most 0.00073.
The roundings to bfloat16 on the way count: a program that leaves them out, or rounds other values in their place, can miss the bound.
Values may be sent and summed in bfloat16 or wider, within the bound.
A program may use at most 64 MiB of HBM per device.

v0:
```python
import functools

import jax
import jax.numpy as jnp
from jax import lax
from jax.sharding import Mesh
from jax.sharding import PartitionSpec as P

D = 5120
FF_WIN = 13312
ROW_COL = ("row_0", "row_1", "col_0", "col_1")
ROW = ("row_0", "row_1")
COL = ("col_0", "col_1")


def by_axis(array, axes):
    return functools.reduce(lax.psum, axes, array)


def gram_rows(left, right):
    return lax.dot_general(
        left, right, (((1,), (1,)), ((), ())), preferred_element_type=jnp.float32
    )


def shards(momentum, gradient):
    new_momentum = 0.95 * momentum + gradient
    squares = by_axis(jnp.sum(new_momentum * new_momentum), ROW_COL)
    normed = new_momentum / (jnp.sqrt(3.0 * squares / D) + 1e-07)
    rounded = normed.astype(jnp.bfloat16)
    gathered = lax.all_gather(rounded, ROW, axis=0, tiled=True)
    partial_value = gram_rows(rounded, gathered)
    gram = lax.psum(partial_value, COL)
    gram_rounded = gram.astype(jnp.bfloat16)
    product = jnp.dot(gram_rounded, gathered, preferred_element_type=jnp.float32)
    update = (1.5 * normed - 0.5 * product) * jnp.sqrt(jnp.float32(3 * FF_WIN))
    return (new_momentum, update)


def solution(mesh):
    torus = Mesh(mesh.devices.reshape(4, 8, 4, 2), ("row_0", "row_1", "col_0", "col_1"))
    return jax.shard_map(
        shards,
        mesh=torus,
        in_specs=(P(ROW, COL), P(ROW, COL)),
        out_specs=(P(ROW, COL), P(ROW, COL)),
        check_vma=False,
    )
```

profile of v0, /device:TPU:25, one launch (start us, length us, event | category | flops | bytes accessed | tf_op | source)
XLA Modules:
  0.0 273.7 jit_solution(8420792981213836205)
XLA Ops:
  7.2 0.0 all-gather.2.cloned.1.call-start
  7.2 2.4 multiply_reduce_fusion
  9.6 0.0 copy-start
  9.6 9.1 %psum.35 = f32[]{:T(128)} all-reduce(f32[]{:T(128)} %get-tuple-element.2), channel_id=1, replica_groups=mesh['row_0'=4,'row_1'=8,'col_0'=4,'col_1'=2] {'row_0'}, use_global_device_ids=true, to_apply=%region_1.0 | all-reduce | flops 1 | bytes 8 | tf_op jit(solution)/shard_map/psum | solution.py:17
  18.7 16.9 %psum.36 = f32[]{:T(128)} all-reduce(f32[]{:T(128)} %psum.35), channel_id=1, replica_groups=mesh['row_0'=4,'row_1'=8,'col_0'=4,'col_1'=2] {'row_1'}, use_global_device_ids=true, to_apply=%region_2.0 | all-reduce | flops 1 | bytes 8 | tf_op jit(solution)/shard_map/psum | solution.py:17
  35.6 6.4 %psum.37 = f32[]{:T(128)} all-reduce(f32[]{:T(128)} %psum.36), channel_id=1, replica_groups=mesh['row_0'=4,'row_1'=8,'col_0'=4,'col_1'=2] {'col_0'}, use_global_device_ids=true, to_apply=%region_3.0 | all-reduce | flops 1 | bytes 8 | tf_op jit(solution)/shard_map/psum | solution.py:17
  41.9 10.9 %psum.38 = f32[]{:T(128)} all-reduce(f32[]{:T(128)} %psum.37), channel_id=1, replica_groups=mesh['row_0'=4,'row_1'=8,'col_0'=4,'col_1'=2] {'col_1'}, use_global_device_ids=true, to_apply=%region_4.0 | all-reduce | flops 1 | bytes 8 | tf_op jit(solution)/shard_map/psum | solution.py:17
  53.5 0.9 fusion.3
  54.4 0.0 all-gather.2.cloned.1.call-update
  54.4 0.0 copy-done
  54.4 136.6 %all-gather.2.cloned.1.call-done = bf16[5120,1664]{1,0:T(8,128)(2,1)} async-done(((bf16[160,1664]{1,0:T(8,128)(2,1)}), bf16[5120,1664]{1,0:T(8,128)(2,1)}) %all-gather.2.cloned.1.call-update) | async-done | bytes 17039376 | tf_op jit(solution)/shard_map/all_gather | solution.py:31
  191.0 9.3 %fusion.4 = f32[160,5120]{1,0:T(8,128)S(1)} fusion(bf16[160,1664]{1,0:T(8,128)(2,1)} %fusion.3, bf16[5120,1664]{1,0:T(8,128)(2,1)} %all-gather.2.cloned.1.call-done), kind=kOutput, calls=%fused_computation.8 | convolution fusion | flops 2726297600 | bytes 20848640 | tf_op jit(solution)/shard_map/dot_general | solution.py:21
  200.3 55.8 %all-reduce.1 = bf16[160,5120]{1,0:T(8,128)(2,1)} all-reduce(f32[160,5120]{1,0:T(8,128)S(1)} %fusion.4), channel_id=1, replica_groups=mesh['row_0'=4,'row_1'=8,'col_0'=4,'col_1'=2] {'col_0','col_1'}, use_global_device_ids=true, to_apply=%region_5.0 | all-reduce | flops 819200 | bytes 4915200 | tf_op jit(solution)/shard_map/psum | solution.py:33
  256.1 10.8 %fusion.1 = f32[160,1664]{1,0:T(8,128)} fusion(bf16[5120,1664]{1,0:T(8,128)(2,1)} %all-gather.2.cloned.1.call-done, bf16[160,5120]{1,0:T(8,128)(2,1)} %all-reduce.1, f32[160,1664]{1,0:T(8,128)} %copy-done, f32[]{:T(128)S(6)} %add.17), kind=kOutput, calls=%fused_computation.2 | convolution fusion | flops 2727628800 | bytes 20807684 | tf_op jit(solution)/shard_map/dot_general | solution.py:35
Async XLA Ops:
  7.2 183.8 %all-gather.2.cloned.1.call-start = ((), (), s32[]{:S(2)}) async-start(), calls=%async_computation | async-start | bytes 17571840 | tf_op jit(solution)/shard_map/all_gather | solution.py:31
  9.6 44.8 %copy-start = (f32[160,1664]{1,0:T(8,128)}, f32[160,1664]{1,0:T(8,128)S(1)}, u32[]{:S(2)}) copy-start(f32[160,1664]{1,0:T(8,128)S(1)} %get-tuple-element.3) | copy-start | bytes 3194884
Sparse Core Ops, SparseCore 0:
  54.6 136.4 all-gather.1
where the time goes:
time: 274 us
  waiting for transfers between devices  137 us (50%)
  blocking collectives  99 us (36%)
  matrix products  20 us (7%)
  between operations  14.7 us (5%)
  other arithmetic  3.3 us (1%)
    all_gather x1, waiting for transfers between devices, shards(): gathered = lax.all_gather(rounded, ROW, axis=0, tiled=True)  137 us
    psum x1, blocking collectives, shards(): gram = lax.psum(partial_value, COL)  55.8 us
    psum x4, blocking collectives, by_axis(): return functools.reduce(lax.psum, axes, array)  43.2 us
    dot_general x1, matrix products, shards(): jnp.dot(gram_rounded, gathered, preferred_element_type=jnp.float32)  10.8 us
    dot_general x1, matrix products, gram_rows(): lax.dot_general(left, right, (((1,), (1,)), ((), ())), preferred_element_...  9.28 us
  transfers between devices with their start and end apart: 1, of which 1 were waited for; matrix products, arithmetic and copies ran while one was open for 0% of the time, Pallas kernels for 0%

commit v1 on v0

v1 whole, which is shorter than its diff:
```python
import functools

import jax
import jax.numpy as jnp
from jax import lax
from jax.experimental import pallas as pl
from jax.experimental.pallas import tpu as pltpu
from jax.sharding import Mesh
from jax.sharding import PartitionSpec as P

D = 5120
FF_WIN = 13312
ROW = ("row_0", "row_1")
COL = ("col_0", "col_1")
X, Z, Y, CORE = 4, 8, 4, 2
ROWS, COLS = D // (X * Z), FF_WIN // (Y * CORE)
HALF = ROWS // 2
A_ROWS, B_ROWS = X * ROWS, Z * ROWS
F32, BF16 = jnp.float32, jnp.bfloat16
GAIN = (3 * FF_WIN) ** 0.5
Z_UP = (0, 1, 3, 5, 7)
Z_DOWN = (0, 2, 4, 6, 7)
X_UP = (0, 1, 3)
X_DOWN = (0, 2, 3)
COLS_X = 1152
COLS_Z = COLS - COLS_X
STEPS = tuple((at, min(256, COLS_X - at)) for at in range(0, COLS_X, 256))


def kernel(
    nm_ref, update_ref,
    tiles, early, early_z, early_x, rb, ra, gt, from_core, half, y_send, y_recv, y_wide, gf, ga, u, u_send, u_mid, u_recv, w, w_send, w_recv,
    done, tile_recv, e_recv, z_recv, x_recv, g_recv, u_rsem, w_rsem,
):
    x, z = lax.axis_index("row_0"), lax.axis_index("row_1")
    y, core = lax.axis_index("col_0"), lax.axis_index("col_1")
    def copy_to(src, dst, send_sem, recv_sem, **where):
        return pltpu.make_async_remote_copy(
            src_ref=src, dst_ref=dst, send_sem=send_sem, recv_sem=recv_sem,
            device_id=where, device_id_type=pl.DeviceIdType.MESH,
        )

    def send(*args, **where):
        copy_to(*args, **where).start()

    def arrive(dst, recv_sem):
        copy_to(dst, dst, recv_sem, recv_sem, col_1=1 - core).wait_recv()

    def sent(src, send_sem):
        copy_to(src, src, send_sem, send_sem, col_1=1 - core).wait_send()

    line_z = [dict(row_1=lax.rem(z + d, Z)) for d in range(1, Z)]
    line_x = [dict(row_0=lax.rem(x + d, X)) for d in range(1, X)]
    column = y * CORE + core
    line_c = []
    for d in range(1, Y * CORE):
        other = lax.rem(column + d, Y * CORE)
        line_c.append(dict(col_0=other // CORE, col_1=lax.rem(other, CORE)))
    partners = line_z + line_x + line_c

    barrier = pltpu.get_barrier_semaphore()
    for where in partners:
        pl.semaphore_signal(barrier, inc=1, device_id=where, device_id_type=pl.DeviceIdType.MESH)

    def add_square(i, total):
        rows = nm_ref[pl.ds(pl.multiple_of(i * 8, 8), 8), :]
        return total + rows * rows

    by_lane = lax.fori_loop(0, ROWS // 8, add_square, jnp.zeros((8, COLS), F32))
    tile = by_lane[:, 0:128]
    for at in range(128, COLS, 128):
        tile = tile + by_lane[:, at : at + 128]
    tile = jnp.sum(tile, axis=0, keepdims=True)
    pl.semaphore_wait(barrier, len(partners))

    up_z, down_z = dict(row_1=lax.rem(z + 1, Z)), dict(row_1=lax.rem(z + Z - 1, Z))
    up_x, down_x = dict(row_0=lax.rem(x + 1, X)), dict(row_0=lax.rem(x + X - 1, X))

    base = 0
    for stage, (me, line, size) in enumerate(((z, line_z, Z), (x, line_x, X), (column, line_c, Y * CORE))):
        tiles[base + me] = tile
        for where in line:
            send(tiles.at[base + me], tiles.at[base + me], done.at[0], tile_recv.at[stage], **where)
        if stage == 0:
            for chunk in range(2):
                for at in range(0, HALF, 16):
                    value = nm_ref[chunk * HALF + at : chunk * HALF + at + 16, :]
                    high = value.astype(BF16)
                    early[chunk, 0, at : at + 16, :] = high
                    early[chunk, 1, at : at + 16, :] = (value - high.astype(F32)).astype(BF16)
            for flow in range(2):
                send(early.at[flow], early_z.at[flow], done.at[1], e_recv.at[0, flow], **(down_z, up_z)[flow])
        if stage == 1:
            for flow in range(2):
                send(early.at[flow], early_x.at[flow], done.at[10], e_recv.at[1, flow], **(down_x, up_x)[flow])
        arrive(tiles.at[pl.ds(base, size - 1)], tile_recv.at[stage])
        tile = tiles[base]
        for k in range(1, size):
            tile = tile + tiles[base + k]
        base += size

    squares = jnp.sum(tile, axis=1, keepdims=True)
    scale = jnp.sqrt(3.0 * squares / D) + 1e-07

    def cast_rows(i, _):
        at = pl.ds(pl.multiple_of(i * 16, 16), 16)
        rounded = (nm_ref[at, :] / scale).astype(BF16)
        rb[at, :] = rounded
        ra[at, :] = rounded
        return 0

    lax.fori_loop(0, ROWS // 16, cast_rows, 0)

    def part(ref, slot, chunk):
        return ref.at[pl.ds(slot * ROWS + chunk * HALF, HALF), :]

    def z_hop(flow, k, chunk):
        slots = (Z_UP, Z_DOWN)[flow]
        send(
            part(rb, slots[k - 1], chunk), part(rb, slots[k], chunk),
            done.at[2], z_recv.at[flow, k - 1, chunk], **(down_z, up_z)[flow],
        )

    def x_hop(flow, k, chunk):
        slots = (X_UP, X_DOWN)[flow]
        send(
            part(ra, slots[k - 1], chunk), part(ra, slots[k], chunk),
            done.at[3], x_recv.at[flow, k - 1, chunk], **(down_x, up_x)[flow],
        )

    def join(pair, ref, slot, chunk):
        for at in range(0, HALF, 16):
            value = pair[0, at : at + 16, :].astype(F32) + pair[1, at : at + 16, :].astype(F32)
            begin = slot * ROWS + chunk * HALF + at
            ref[begin : begin + 16, :] = (value / scale).astype(BF16)

    def z_in(flow, k, chunk):
        slot = (Z_UP, Z_DOWN)[flow][k]
        if k == 1 and chunk == flow:
            arrive(early_z.at[flow], e_recv.at[0, flow])
            join(early_z.at[flow], rb, slot, chunk)
        else:
            arrive(part(rb, slot, chunk), z_recv.at[flow, k - 1, chunk])
        if k < 3 or (k == 3 and chunk == flow):
            z_hop(flow, k + 1, chunk)

    def x_in(flow, k, chunk):
        slot = (X_UP, X_DOWN)[flow][k]
        if k == 1 and chunk == flow:
            arrive(early_x.at[flow], e_recv.at[1, flow])
            join(early_x.at[flow], ra, slot, chunk)
            x_hop(flow, 2, chunk)
        else:
            arrive(part(ra, slot, chunk), x_recv.at[flow, k - 1, chunk])

    y_first, y_second = y + 1 - 2 * lax.rem(y, 2), 3 - y
    mine, theirs = core * HALF, (1 - core) * HALF

    def half_of(ref, slot, which):
        return ref.at[pl.ds(pl.multiple_of(slot * ROWS + which, HALF), HALF), :]

    def gram(low, high):
        left = rb[low * ROWS : high * ROWS, :]
        for at in range(0, A_ROWS, 128):
            gt[low * ROWS : high * ROWS, at : at + 128] = lax.dot_general(
                left, ra[at : at + 128, :], (((1,), (1,)), ((), ())), preferred_element_type=F32
            )
        for slot in range(low, high):
            send(half_of(gt, slot, theirs), from_core.at[slot], done.at[4], g_recv.at[0, slot], col_1=1 - core)

    def y_parts(slot):
        split = HALF // 2 if slot == 0 else 48
        return ((0, split, (y_first, y_second)), (split, HALF - split, (y_second, y_first)))

    def y_send_of(slot, step):
        for at, count, order in y_parts(slot):
            if slot == 0:
                src, dst = half.at[8 * step, pl.ds(at, count), :], y_wide.at[step, pl.ds(at, count), :]
            else:
                src, dst = y_send.at[step, slot, pl.ds(at, count), :], y_recv.at[step, slot, pl.ds(at, count), :]
            send(src, dst, done.at[5 if slot == 0 else 6], g_recv.at[1 + step, slot], col_0=order[step])

    def y_arrive(slot, step):
        arrive(y_wide.at[step] if slot == 0 else y_recv.at[step, slot], g_recv.at[1 + step, slot])

    def sum_cores(slot):
        arrive(from_core.at[slot], g_recv.at[0, slot])
        value = half_of(gt, slot, mine)[...] + from_core[slot]
        half[slot] = value
        if slot:
            y_send[0, slot] = value
        y_send_of(slot, 0)

    def sum_first(slot):
        y_arrive(slot, 0)
        if slot == 0:
            half[8] = half[0] + y_wide[0]
        else:
            value = half[slot] + y_recv[0, slot]
            half[slot] = value
            y_send[1, slot] = value
        y_send_of(slot, 1)

    def sum_second(slot):
        y_arrive(slot, 1)
        if slot == 0:
            value = half[8] + y_wide[1]
        else:
            value = half[slot] + y_recv[1, slot]
        half_of(gf, slot, mine)[...] = value.astype(BF16)
        send(half_of(gf, slot, mine), half_of(gf, slot, mine), done.at[7], g_recv.at[3, slot], col_1=1 - core)

    def turn(slot):
        arrive(half_of(gf, slot, theirs), g_recv.at[3, slot])
        ga[slot] = gf[slot * ROWS : (slot + 1) * ROWS, :].T

    def multiply_z(low, high):
        rows = slice(low * ROWS, high * ROWS)
        w[rows, :] = jnp.dot(gf[rows, :], ra[:, COLS_X:], preferred_element_type=F32)

    def multiply(low, high, first):
        for at, width in STEPS:
            total = None if first else u[:, at : at + width]
            for slot in range(low, high):
                term = jnp.dot(
                    ga[slot], rb[slot * ROWS : (slot + 1) * ROWS, at : at + width], preferred_element_type=F32
                )
                total = term if total is None else total + term
            u[:, at : at + width] = total

    def w_at(flow, chunk, step):
        return flow * 7 + (step if chunk == flow else 3 + step)

    def w_hop(flow, chunk, step):
        begin = (Z_UP, Z_DOWN)[flow][4 - step] * ROWS + chunk * HALF
        value = w[begin : begin + HALF, :]
        at = w_at(flow, chunk, step)
        if step > (0 if chunk == flow else 1):
            arrive(w_recv.at[at - 1], w_rsem.at[flow, chunk, step - 1])
            value = value + w_recv[at - 1]
        w_send[at] = value
        send(w_send.at[at], w_recv.at[at], done.at[9], w_rsem.at[flow, chunk, step], **(up_z, down_z)[flow])

    for flow in range(2):
        z_hop(flow, 1, 1 - flow)
        x_hop(flow, 1, 1 - flow)
    for flow in range(2):
        z_in(flow, 1, flow)
    for flow in range(2):
        x_in(flow, 1, flow)
    for flow in range(2):
        z_in(flow, 1, 1 - flow)
    for flow in range(2):
        x_in(flow, 1, 1 - flow)
    for flow in range(2):
        z_in(flow, 2, flow)
    for flow in range(2):
        x_in(flow, 2, flow)
    gram(0, 1)
    gram(1, 3)
    sum_cores(0)
    for flow in range(2):
        z_in(flow, 2, 1 - flow)
    gram(3, 5)
    sum_cores(1)
    sum_cores(2)
    sum_first(0)
    sum_cores(3)
    sum_cores(4)
    for flow in range(2):
        z_in(flow, 3, flow)
    sum_first(1)
    sum_first(2)
    for flow in range(2):
        z_in(flow, 3, 1 - flow)
    gram(5, 7)
    sum_first(3)
    sum_first(4)
    sum_cores(5)
    sum_cores(6)
    sum_second(0)
    sum_second(1)
    sum_second(2)
    for flow in range(2):
        z_in(flow, 4, flow)
    gram(7, 8)
    sum_cores(7)
    sum_first(5)
    sum_first(6)
    sum_second(3)
    sum_second(4)
    turn(0)
    turn(1)
    turn(2)
    multiply(0, 2, True)
    multiply_z(0, 3)
    sum_first(7)
    turn(3)
    turn(4)
    multiply(2, 5, False)
    multiply_z(3, 5)
    sum_second(5)
    sum_second(6)
    sum_second(7)
    turn(5)
    turn(6)
    multiply_z(5, 7)
    for flow in range(2):
        w_hop(flow, 1 - flow, 1)
    turn(7)

    def u_rows(slot, chunk):
        return u[slot * ROWS + chunk * HALF : slot * ROWS + (chunk + 1) * HALF, :]

    def finish(slot):
        rows = slice(slot * ROWS, (slot + 1) * ROWS)
        total = u[rows, :]
        for late in range(5, Z):
            right = rb[late * ROWS : (late + 1) * ROWS, :COLS_X]
            total = total + jnp.dot(ga[late, rows, :], right, preferred_element_type=F32)
        u[rows, :] = total

    finish(3)
    for flow in range(2):
        u_send[2 * flow] = u_rows(3, flow)
        send(u_send.at[2 * flow], u_mid.at[flow], done.at[8], u_rsem.at[flow, 0], **(up_x, down_x)[flow])
    multiply_z(7, 8)
    for flow in range(2):
        w_hop(flow, flow, 0)
    for flow in range(2):
        finish(1 + flow)
        u_send[2 * flow + 1] = u_rows(1 + flow, 1 - flow)
        send(
            u_send.at[2 * flow + 1], u_recv.at[flow, 1 - flow],
            done.at[8], u_rsem.at[flow, 1], **(up_x, down_x)[flow],
        )
    for flow in range(2):
        w_hop(flow, 1 - flow, 2)
    for flow in range(2):
        w_hop(flow, flow, 1)
    finish(0)
    update_ref[:, :COLS_X] = 1.5 * (nm_ref[:, :COLS_X] / scale) - 0.5 * u[0:ROWS, :]
    update_ref[:, COLS_X:] = 1.5 * (nm_ref[:, COLS_X:] / scale) - 0.5 * w[0:ROWS, :]
    for flow in range(2):
        arrive(u_mid.at[flow], u_rsem.at[flow, 0])
        u_send[4 + flow] = u_rows(1 + flow, flow) + u_mid[flow]
        send(
            u_send.at[4 + flow], u_recv.at[flow, flow],
            done.at[8], u_rsem.at[flow, 2], **(up_x, down_x)[flow],
        )
    for flow in range(2):
        w_hop(flow, 1 - flow, 3)
    for flow in range(2):
        w_hop(flow, flow, 2)
    for flow in range(2):
        w_hop(flow, flow, 3)
    for flow in range(2):
        arrive(u_recv.at[flow, 1 - flow], u_rsem.at[flow, 1])
    for chunk in range(2):
        rows = slice(chunk * HALF, (chunk + 1) * HALF)
        others = jnp.zeros((HALF, COLS_Z), F32)
        for flow in range(2):
            arrive(w_recv.at[w_at(flow, chunk, 3)], w_rsem.at[flow, chunk, 3])
            others = others + w_recv[w_at(flow, chunk, 3)]
        update_ref[rows, COLS_X:] = (update_ref[rows, COLS_X:] - 0.5 * others) * GAIN
    for flow in range(2):
        arrive(u_recv.at[flow, flow], u_rsem.at[flow, 2])
    for chunk in range(2):
        rows = slice(chunk * HALF, (chunk + 1) * HALF)
        others = u_recv[0, chunk] + u_recv[1, chunk]
        update_ref[rows, :COLS_X] = (update_ref[rows, :COLS_X] - 0.5 * others) * GAIN

    for group, src in enumerate((
        tiles.at[pl.ds(0, len(partners))], early, rb.at[pl.ds(0, 12 * HALF), :], ra.at[pl.ds(0, 4 * HALF), :],
        from_core, y_wide, y_send.at[:, pl.ds(1, Z - 1)], gf.at[pl.ds(0, Z * HALF), :], u_send, w_send, early,
    )):
        sent(src, done.at[group])


def products(new_momentum):
    dma = pltpu.SemaphoreType.DMA
    return pl.pallas_call(
        kernel,
        out_shape=pltpu.VMEM((ROWS, COLS), F32),
        in_specs=[pl.BlockSpec(memory_space=pltpu.VMEM)],
        out_specs=pl.BlockSpec(memory_space=pltpu.VMEM),
        scratch_shapes=[
            pltpu.VMEM((Z + X + Y * CORE, 1, 128), F32),
            pltpu.VMEM((2, 2, HALF, COLS), BF16),
            pltpu.VMEM((2, 2, HALF, COLS), BF16),
            pltpu.VMEM((2, 2, HALF, COLS), BF16),
            pltpu.VMEM((B_ROWS, COLS), BF16),
            pltpu.VMEM((A_ROWS, COLS), BF16),
            pltpu.VMEM((B_ROWS, A_ROWS), F32),
            pltpu.VMEM((Z, HALF, A_ROWS), F32),
            pltpu.VMEM((Z + 1, HALF, A_ROWS), F32),
            pltpu.VMEM((2, Z, HALF, A_ROWS), F32),
            pltpu.VMEM((2, Z, HALF, A_ROWS), F32),
            pltpu.VMEM((2, HALF, A_ROWS), F32),
            pltpu.VMEM((B_ROWS, A_ROWS), BF16),
            pltpu.VMEM((Z, A_ROWS, ROWS), BF16),
            pltpu.VMEM((A_ROWS, COLS_X), F32),
            pltpu.VMEM((6, HALF, COLS_X), F32),
            pltpu.VMEM((2, HALF, COLS_X), F32),
            pltpu.VMEM((2, 2, HALF, COLS_X), F32),
            pltpu.VMEM((B_ROWS, COLS_Z), F32),
            pltpu.VMEM((14, HALF, COLS_Z), F32),
            pltpu.VMEM((14, HALF, COLS_Z), F32),
            dma((11,)), dma((3,)), dma((2, 2)), dma((2, 4, 2)), dma((2, 2, 2)), dma((4, Z)), dma((2, 3)), dma((2, 2, 4)),
        ],
        compiler_params=pltpu.CompilerParams(
            collective_id=0, has_side_effects=True, vmem_limit_bytes=56 * 1024 * 1024
        ),
    )(pltpu.with_memory_space_constraint(new_momentum, pltpu.VMEM))


def shards(momentum, gradient):
    new_momentum = 0.95 * momentum + gradient
    update = products(new_momentum)
    return (new_momentum, update)


def solution(mesh):
    torus = Mesh(mesh.devices.reshape(X, Z, Y, CORE), ROW + COL)
    return jax.shard_map(
        shards,
        mesh=torus,
        in_specs=(P(ROW, COL), P(ROW, COL)),
        out_specs=(P(ROW, COL), P(ROW, COL)),
        check_vma=False,
    )
```

time: 274 us -> 111 us (0.41)
  waiting for transfers between devices: 137 us -> 0 us
  Pallas kernels: 0 us -> 106 us
  blocking collectives: 99 us -> 0 us
  matrix products: 20 us -> 0 us
  between operations: 14.7 us -> 0.65 us
    all_gather x1 -> x0, waiting for transfers between devices: 137 us -> none  [shards(): gathered = lax.all_gather(rounded, ROW, axis=0, tiled=True)]
    pallas_call x0 -> x1, Pallas kernels: none -> 106 us  [products(): pl.pallas_call(kernel, out_shape=pltpu.VMEM((ROWS, COLS), F32), in_specs=...]
    psum x5 -> x0, blocking collectives: 99 us -> none  [the longest x1 55.8 us: shards(): gram = lax.psum(partial_value, COL)]
    dot_general x2 -> x0, matrix products: 20 us -> none  [the longest x1 10.8 us: shards(): jnp.dot(gram_rounded, gathered, preferred_element_type=jnp.float32)]
  transfers between devices with their start and end apart: 1 -> 0, of which waited for: 1 -> 0; matrix products, arithmetic and copies ran while one was open for 0% -> 0% of each run, Pallas kernels for 0% -> 0%
where the time goes in v1:
time: 111 us; the launch traced here: 109 us
  Pallas kernels  106 us (95%)
  other arithmetic  1.67 us (2%)
    pallas_call x1, Pallas kernels, products(): pl.pallas_call(kernel, out_shape=pltpu.VMEM((ROWS, COLS), F32), in_specs=...  106 us

profile of v1, /device:TPU:25, one launch (start us, length us, event | category | flops | bytes accessed | tf_op | source)
XLA Modules:
  0.0 109.0 jit_solution(2646293350996479290)
XLA Ops:
  0.6 1.7 %multiply_add_fusion.nm_ref = f32[160,1664]{1,0:T(8,128)S(1)} fusion(f32[160,1664]{1,0:T(8,128)} %param.3, f32[160,1664]{1,0:T(8,128)} %param.2), kind=kLoop, calls=%fused_computation | loop fusion | flops 532480 | bytes 3194880 | tf_op jit(solution)/shard_map/add | solution.py:418
  2.3 0.0 copy-start
  2.3 105.7 %shard_map.41 = f32[160,1664]{1,0:T(8,128)S(1)} custom-call(f32[160,1664]{1,0:T(8,128)S(1)} %multiply_add_fusion.nm_ref), custom_call_target="tpu_custom_call" | custom-call | tf_op jit(solution)/shard_map/pallas_call | solution.py:382
  108.0 1.0 copy.5
  109.0 0.0 copy-done
Async XLA Ops:
  2.3 106.7 %copy-start = (f32[160,1664]{1,0:T(8,128)}, f32[160,1664]{1,0:T(8,128)S(1)}, u32[]{:S(2)}) copy-start(f32[160,1664]{1,0:T(8,128)S(1)} %multiply_add_fusion.nm_ref) | copy-start | bytes 3194884
